TPU v7x, 32 devices: a whole 2x2x4 slice. The times are simulated.
32 devices in a mesh: row: 8 (over y, x, core), col: 4 (over z).
Axes of the slice: x: 2, y: 2, z: 4, core: 2. Of those that a mesh axis runs over, the one named last changes fastest.
Arguments:
- act_tiles: bfloat16 [3072, 2048], P('row', 'col'), may hold values from -6 to 6
- up_tiles: bfloat16 [2048, 3584], P('row', 'col'), may hold values from -0.125 to 0.125
Outputs:
- hidden_act: bfloat16 [3072, 3584], P('row', 'col')
All inputs are finite; a program needn't handle non-finite values.
Results may differ from a plain program's by a relative error of at most 0.001.
Values may be sent and summed in bfloat16 or wider, within the bound.
A program may use at most 64 MiB of HBM per device.

v0:
```python
import jax
import jax.numpy as jnp
from jax import lax
from jax.sharding import PartitionSpec as P


def passed_along(block, axis, distance):
    devices = range(lax.axis_size(axis))
    route = [((i - distance) % len(devices), i) for i in devices]
    return lax.ppermute(block, axis, route)


def body(act_tiles, up_tiles):
    col_count = lax.axis_size("col")
    following = passed_along(up_tiles, "row", -1)
    pair_first = jnp.concatenate([up_tiles, following], 0)
    summed = jnp.dot(act_tiles, pair_first, preferred_element_type=jnp.float32)

    def advance(step_index, state_tuple):
        act_now, pair_now, running = state_tuple
        act_now = passed_along(act_now, "col", -1)
        pair_now = passed_along(pair_now, "row", -2)
        running = running + jnp.dot(act_now, pair_now, preferred_element_type=jnp.float32)
        return (act_now, pair_now, running)

    final_state = lax.fori_loop(0, col_count - 1, advance, (act_tiles, pair_first, summed))
    summed = final_state[2]
    return jax.nn.silu(summed).astype(jnp.bfloat16)


def solution(mesh):
    return jax.shard_map(
        body,
        mesh=mesh,
        in_specs=(P("row", "col"), P("row", "col")),
        out_specs=P("row", "col"),
        check_vma=False,
    )
```

profile of v0, /device:TPU:0, one launch (start us, length us, event | category | flops | bytes accessed | tf_op | source)
XLA Modules:
  0.0 86.5 jit_solution(6492096794501560423)
XLA Ops:
  0.0 1.0 %copy.19 = bf16[384,512]{1,0:T(8,128)(2,1)S(1)} copy(bf16[384,512]{1,0:T(8,128)(2,1)} %param.4) | data formatting | bytes 786432
  1.0 3.4 %collective-permute-start.2 = (bf16[256,896]{1,0:T(8,128)(2,1)}, bf16[256,896]{1,0:T(8,128)(2,1)S(1)}, u32[]{:S(2)}, u32[]{:S(2)}) collective-permute-start(bf16[256,896]{1,0:T(8,128)(2,1)} %param.5), channel_id=1, source_target_pairs={{4,0},{8,4},{12,8},{16,12},{20,16},{24,20},{28,24},{0,28},{5,1},{9... | collective-permute-start | bytes 1376264 | tf_op jit(solution)/shard_map/ppermute | solution.py:10
  4.4 1.1 %constant_dynamic-update-slice_fusion.1 = bf16[512,896]{1,0:T(8,128)(2,1)S(1)} fusion(bf16[256,896]{1,0:T(8,128)(2,1)} %param.5), kind=kLoop, calls=%fused_computation.4 | loop fusion | bytes 917504
  5.5 5.2 %collective-permute-done.2 = bf16[256,896]{1,0:T(8,128)(2,1)S(1)} collective-permute-done((bf16[256,896]{1,0:T(8,128)(2,1)}, bf16[256,896]{1,0:T(8,128)(2,1)S(1)}, u32[]{:S(2)}, u32[]{:S(2)}) %collective-permute-start.2) | collective-permute-done | bytes 458784 | tf_op jit(solution)/shard_map/ppermute | solution.py:10
  10.7 0.9 %copy-done = bf16[512,896]{1,0:T(8,128)(2,1)} copy-done((bf16[512,896]{1,0:T(8,128)(2,1)}, bf16[512,896]{1,0:T(8,128)(2,1)S(1)}, u32[]{:S(2)}) %copy-start) | copy-done | bytes 917528
  11.7 0.7 convolution_bitcast_fusion
  12.8 72.5 %while.14 = (s32[]{:T(128)}, bf16[384,512]{1,0:T(8,128)(2,1)S(1)}, bf16[512,896]{1,0:T(8,128)(2,1)}, f32[384,896]{1,0:T(8,128)S(1)}, s32[]{:T(128)}) while((s32[]{:T(128)}, bf16[384,512]{1,0:T(8,128)(2,1)S(1)}, bf16[512,896]{1,0:T(8,128)(2,1)}, f32[384,896]{1,0:T(8,128)S(1)}, s32[]{:T(128)}) %tuple.22), condition=%wide.region_1.0_spmd, body=%wide.region_0.0_spmd.sunk | while | flops 352665600 | bytes 11927693 | solution.py:26
  13.4 3.6 %collective-permute-start = (bf16[384,512]{1,0:T(8,128)(2,1)S(1)}, bf16[384,512]{1,0:T(8,128)(2,1)S(1)}, u32[]{:S(2)}, u32[]{:S(2)}) collective-permute-start(bf16[384,512]{1,0:T(8,128)(2,1)S(1)} %get-tuple-element.71), channel_id=1, source_target_pairs={{1,0},{2,1},{3,2},{0,3},{5,4},{6,5},{7,6},{4,7},{9,8},{10,9},{11,1... | collective-permute-start | bytes 1179656 | tf_op jit(solution)/shard_map/while/body/eval_jaxpr/ppermute | solution.py:10
  17.0 8.2 %collective-permute-done = bf16[384,512]{1,0:T(8,128)(2,1)S(1)} collective-permute-done((bf16[384,512]{1,0:T(8,128)(2,1)S(1)}, bf16[384,512]{1,0:T(8,128)(2,1)S(1)}, u32[]{:S(2)}, u32[]{:S(2)}) %collective-permute-start) | collective-permute-done | bytes 393248 | tf_op jit(solution)/shard_map/while/body/eval_jaxpr/ppermute | solution.py:10
  25.3 10.4 %collective-permute-done.1 = bf16[512,896]{1,0:T(8,128)(2,1)S(1)} collective-permute-done((bf16[512,896]{1,0:T(8,128)(2,1)}, bf16[512,896]{1,0:T(8,128)(2,1)S(1)}, u32[]{:S(2)}, u32[]{:S(2)}) %collective-permute-start.1) | collective-permute-done | bytes 917536 | tf_op jit(solution)/shard_map/while/body/eval_jaxpr/ppermute | solution.py:10
  35.7 0.9 %copy.15 = bf16[512,896]{1,0:T(8,128)(2,1)} copy(bf16[512,896]{1,0:T(8,128)(2,1)S(1)} %collective-permute-done.1) | data formatting | bytes 1835008 | tf_op jit(solution)/shard_map/while
  36.6 0.6 convolution_add_fusion.2
  37.8 3.6 %collective-permute-start = (bf16[384,512]{1,0:T(8,128)(2,1)S(1)}, bf16[384,512]{1,0:T(8,128)(2,1)S(1)}, u32[]{:S(2)}, u32[]{:S(2)}) collective-permute-start(bf16[384,512]{1,0:T(8,128)(2,1)S(1)} %get-tuple-element.71), channel_id=1, source_target_pairs={{1,0},{2,1},{3,2},{0,3},{5,4},{6,5},{7,6},{4,7},{9,8},{10,9},{11,1... | collective-permute-start | bytes 1179656 | tf_op jit(solution)/shard_map/while/body/eval_jaxpr/ppermute | solution.py:10
  41.4 9.4 %collective-permute-done = bf16[384,512]{1,0:T(8,128)(2,1)S(1)} collective-permute-done((bf16[384,512]{1,0:T(8,128)(2,1)S(1)}, bf16[384,512]{1,0:T(8,128)(2,1)S(1)}, u32[]{:S(2)}, u32[]{:S(2)}) %collective-permute-start) | collective-permute-done | bytes 393248 | tf_op jit(solution)/shard_map/while/body/eval_jaxpr/ppermute | solution.py:10
  50.8 8.5 %collective-permute-done.1 = bf16[512,896]{1,0:T(8,128)(2,1)S(1)} collective-permute-done((bf16[512,896]{1,0:T(8,128)(2,1)}, bf16[512,896]{1,0:T(8,128)(2,1)S(1)}, u32[]{:S(2)}, u32[]{:S(2)}) %collective-permute-start.1) | collective-permute-done | bytes 917536 | tf_op jit(solution)/shard_map/while/body/eval_jaxpr/ppermute | solution.py:10
  59.4 0.9 %copy.15 = bf16[512,896]{1,0:T(8,128)(2,1)} copy(bf16[512,896]{1,0:T(8,128)(2,1)S(1)} %collective-permute-done.1) | data formatting | bytes 1835008 | tf_op jit(solution)/shard_map/while
  60.3 0.6 convolution_add_fusion.2
  60.9 2.4 %collective-permute-start.1 = (bf16[512,896]{1,0:T(8,128)(2,1)}, bf16[512,896]{1,0:T(8,128)(2,1)S(1)}, u32[]{:S(2)}, u32[]{:S(2)}) collective-permute-start(bf16[512,896]{1,0:T(8,128)(2,1)} %get-tuple-element.72), channel_id=1, source_target_pairs={{8,0},{12,4},{16,8},{20,12},{24,16},{28,20},{0,24},{4,28},{9,1},{1... | collective-permute-start | bytes 2752520 | tf_op jit(solution)/shard_map/while/body/eval_jaxpr/ppermute | solution.py:10
  63.4 3.6 %collective-permute-start = (bf16[384,512]{1,0:T(8,128)(2,1)S(1)}, bf16[384,512]{1,0:T(8,128)(2,1)S(1)}, u32[]{:S(2)}, u32[]{:S(2)}) collective-permute-start(bf16[384,512]{1,0:T(8,128)(2,1)S(1)} %get-tuple-element.71), channel_id=1, source_target_pairs={{1,0},{2,1},{3,2},{0,3},{5,4},{6,5},{7,6},{4,7},{9,8},{10,9},{11,1... | collective-permute-start | bytes 1179656 | tf_op jit(solution)/shard_map/while/body/eval_jaxpr/ppermute | solution.py:10
  67.0 8.5 %collective-permute-done = bf16[384,512]{1,0:T(8,128)(2,1)S(1)} collective-permute-done((bf16[384,512]{1,0:T(8,128)(2,1)S(1)}, bf16[384,512]{1,0:T(8,128)(2,1)S(1)}, u32[]{:S(2)}, u32[]{:S(2)}) %collective-permute-start) | collective-permute-done | bytes 393248 | tf_op jit(solution)/shard_map/while/body/eval_jaxpr/ppermute | solution.py:10
  75.5 8.2 %collective-permute-done.1 = bf16[512,896]{1,0:T(8,128)(2,1)S(1)} collective-permute-done((bf16[512,896]{1,0:T(8,128)(2,1)}, bf16[512,896]{1,0:T(8,128)(2,1)S(1)}, u32[]{:S(2)}, u32[]{:S(2)}) %collective-permute-start.1) | collective-permute-done | bytes 917536 | tf_op jit(solution)/shard_map/while/body/eval_jaxpr/ppermute | solution.py:10
  83.7 0.9 %copy.15 = bf16[512,896]{1,0:T(8,128)(2,1)} copy(bf16[512,896]{1,0:T(8,128)(2,1)S(1)} %collective-permute-done.1) | data formatting | bytes 1835008 | tf_op jit(solution)/shard_map/while
  84.6 0.6 convolution_add_fusion.2
  85.3 1.2 %multiply_convert_fusion = bf16[384,896]{1,0:T(8,128)(2,1)} fusion(f32[384,896]{1,0:T(8,128)S(1)} %get-tuple-element.27), kind=kLoop, calls=%fused_computation.2 | loop fusion | flops 1720320 | bytes 2064384 | tf_op jit(solution)/shard_map/convert_element_type | solution.py:28
  (8 shorter events, 1.7 us)
Async XLA Ops:
  1.0 9.7 %collective-permute-start.2 = (bf16[256,896]{1,0:T(8,128)(2,1)}, bf16[256,896]{1,0:T(8,128)(2,1)S(1)}, u32[]{:S(2)}, u32[]{:S(2)}) collective-permute-start(bf16[256,896]{1,0:T(8,128)(2,1)} %param.5), channel_id=1, source_target_pairs={{4,0},{8,4},{12,8},{16,12},{20,16},{24,20},{28,24},{0,28},{5,1},{9... | collective-permute-start | bytes 1376264 | tf_op jit(solution)/shard_map/ppermute | solution.py:10
  10.7 0.9 %copy-start = (bf16[512,896]{1,0:T(8,128)(2,1)}, bf16[512,896]{1,0:T(8,128)(2,1)S(1)}, u32[]{:S(2)}) copy-start(bf16[512,896]{1,0:T(8,128)(2,1)S(1)} %constant_dynamic-update-slice_fusion) | copy-start | bytes 2752516
  12.8 22.9 %collective-permute-start.1 = (bf16[512,896]{1,0:T(8,128)(2,1)}, bf16[512,896]{1,0:T(8,128)(2,1)S(1)}, u32[]{:S(2)}, u32[]{:S(2)}) collective-permute-start(bf16[512,896]{1,0:T(8,128)(2,1)} %get-tuple-element.72), channel_id=1, source_target_pairs={{8,0},{12,4},{16,8},{20,12},{24,16},{28,20},{0,24},{4,28},{9,1},{1... | collective-permute-start | bytes 2752520 | tf_op jit(solution)/shard_map/while/body/eval_jaxpr/ppermute | solution.py:10
  13.4 11.8 %collective-permute-start = (bf16[384,512]{1,0:T(8,128)(2,1)S(1)}, bf16[384,512]{1,0:T(8,128)(2,1)S(1)}, u32[]{:S(2)}, u32[]{:S(2)}) collective-permute-start(bf16[384,512]{1,0:T(8,128)(2,1)S(1)} %get-tuple-element.71), channel_id=1, source_target_pairs={{1,0},{2,1},{3,2},{0,3},{5,4},{6,5},{7,6},{4,7},{9,8},{10,9},{11,1... | collective-permute-start | bytes 1179656 | tf_op jit(solution)/shard_map/while/body/eval_jaxpr/ppermute | solution.py:10
  37.3 22.1 %collective-permute-start.1 = (bf16[512,896]{1,0:T(8,128)(2,1)}, bf16[512,896]{1,0:T(8,128)(2,1)S(1)}, u32[]{:S(2)}, u32[]{:S(2)}) collective-permute-start(bf16[512,896]{1,0:T(8,128)(2,1)} %get-tuple-element.72), channel_id=1, source_target_pairs={{8,0},{12,4},{16,8},{20,12},{24,16},{28,20},{0,24},{4,28},{9,1},{1... | collective-permute-start | bytes 2752520 | tf_op jit(solution)/shard_map/while/body/eval_jaxpr/ppermute | solution.py:10
  37.8 13.0 %collective-permute-start = (bf16[384,512]{1,0:T(8,128)(2,1)S(1)}, bf16[384,512]{1,0:T(8,128)(2,1)S(1)}, u32[]{:S(2)}, u32[]{:S(2)}) collective-permute-start(bf16[384,512]{1,0:T(8,128)(2,1)S(1)} %get-tuple-element.71), channel_id=1, source_target_pairs={{1,0},{2,1},{3,2},{0,3},{5,4},{6,5},{7,6},{4,7},{9,8},{10,9},{11,1... | collective-permute-start | bytes 1179656 | tf_op jit(solution)/shard_map/while/body/eval_jaxpr/ppermute | solution.py:10
  60.9 22.8 %collective-permute-start.1 = (bf16[512,896]{1,0:T(8,128)(2,1)}, bf16[512,896]{1,0:T(8,128)(2,1)S(1)}, u32[]{:S(2)}, u32[]{:S(2)}) collective-permute-start(bf16[512,896]{1,0:T(8,128)(2,1)} %get-tuple-element.72), channel_id=1, source_target_pairs={{8,0},{12,4},{16,8},{20,12},{24,16},{28,20},{0,24},{4,28},{9,1},{1... | collective-permute-start | bytes 2752520 | tf_op jit(solution)/shard_map/while/body/eval_jaxpr/ppermute | solution.py:10
  63.4 12.1 %collective-permute-start = (bf16[384,512]{1,0:T(8,128)(2,1)S(1)}, bf16[384,512]{1,0:T(8,128)(2,1)S(1)}, u32[]{:S(2)}, u32[]{:S(2)}) collective-permute-start(bf16[384,512]{1,0:T(8,128)(2,1)S(1)} %get-tuple-element.71), channel_id=1, source_target_pairs={{1,0},{2,1},{3,2},{0,3},{5,4},{6,5},{7,6},{4,7},{9,8},{10,9},{11,1... | collective-permute-start | bytes 1179656 | tf_op jit(solution)/shard_map/while/body/eval_jaxpr/ppermute | solution.py:10
where the time goes:
time: 86.7 us; the launch traced here: 86.5 us
  waiting for transfers between devices  58.5 us (67%)
  starting transfers between devices  17.7 us (20%)
  local copies, waits for them, and re-layouts  6.35 us (7%)
  matrix products  2.59 us (3%)
  other arithmetic  1.21 us (1%)
    ppermute x7, waiting for transfers between devices, passed_along(): return lax.ppermute(block, axis, route)  58.5 us
    ppermute x7, starting transfers between devices, passed_along(): return lax.ppermute(block, axis, route)  17.7 us
    unnamed x4, local copies, waits for them, and re-layouts  3.01 us
    while x6, local copies, waits for them, and re-layouts  2.86 us
    dot_general x3, matrix products, advance(): jnp.dot(act_now, pair_now, preferred_element_type=jnp.float32)  1.92 us
  transfers between devices with their start and end apart: 7, of which 7 were waited for; matrix products, arithmetic and copies ran while one was open for 1% of the time, Pallas kernels for 0%

commit v1 on v0

v1 whole, which is shorter than its diff:
```python
import functools

import jax
import jax.numpy as jnp
from jax import lax
from jax.experimental import pallas as pl
from jax.experimental.pallas import tpu as pltpu
from jax.sharding import PartitionSpec as P

MESH = pl.DeviceIdType.MESH


def pieces_of(rows, wanted, multiple):
    return max(n for n in range(1, wanted + 1) if rows % (n * multiple) == 0)


def kernel(grid, counts, a_hbm, w_hbm, out, acts, weights, total, send_a, recv_a, send_w, recv_w, local_sem):
    n_y, n_x, n_col = grid
    n_a, n_w = counts
    n_row = 2 * n_y * n_x
    tokens, width = acts.shape[1:]
    depth = w_hbm.shape[0]
    per = width // depth
    row_a, row_w = tokens // n_a, depth // n_w

    r, c = lax.axis_index("row"), lax.axis_index("col")
    core = lax.rem(r, 2)
    x = lax.rem(r // 2, n_x)
    y = r // (2 * n_x)
    last = n_col - 1

    def row_of(dy, dx, other_core=False):
        which = 1 - core if other_core else core
        return (lax.rem(y + dy, n_y) * n_x + lax.rem(x + dx, n_x)) * 2 + which

    pair = row_of(0, 0, True)
    peers_x = [(0, dx) for dx in range(1, n_x)]
    peers_y = [(dy, 0) for dy in range(1, n_y)]
    diagonal = [(dy, dx) for dy in range(1, n_y) for dx in range(1, n_x)]

    def weight_at(source, owner, k):
        rel = lax.rem(source - owner + n_row, n_row)
        return weights.at[rel // per, pl.ds(pl.multiple_of(lax.rem(rel, per) * depth + k * row_w, row_w), row_w)]

    def weight_copy(source, to, slot, k):
        return pltpu.make_async_remote_copy(
            src_ref=weight_at(source, r, k),
            dst_ref=weight_at(source, to, k),
            send_sem=send_w.at[slot, k],
            recv_sem=recv_w.at[source, k],
            device_id=(to, c),
            device_id_type=MESH,
        )

    def act_copy(source, side, k):
        return pltpu.make_async_remote_copy(
            src_ref=acts.at[source, pl.ds(k * row_a, row_a)],
            dst_ref=acts.at[source, pl.ds(k * row_a, row_a)],
            send_sem=send_a.at[side, source, k],
            recv_sem=recv_a.at[source, k],
            device_id=(r, c + 2 * side - 1),
            device_id_type=MESH,
        )

    own_a = pltpu.make_async_copy(a_hbm, acts.at[c], local_sem.at[0])
    own_w = pltpu.make_async_copy(w_hbm, weights.at[0, pl.ds(0, depth)], local_sem.at[1])
    own_a.start()
    own_w.start()

    barrier = pltpu.get_barrier_semaphore()
    row_peers = [row_of(*p) for p in peers_x + peers_y] + [pair]
    for to in row_peers:
        pl.semaphore_signal(barrier, inc=1, device_id=(to, c), device_id_type=MESH)

    @pl.when(c > 0)
    def _():
        pl.semaphore_signal(barrier, inc=1, device_id=(r, c - 1), device_id_type=MESH)

    @pl.when(c < last)
    def _():
        pl.semaphore_signal(barrier, inc=1, device_id=(r, c + 1), device_id_type=MESH)

    beside = jnp.where(c > 0, 1, 0) + jnp.where(c < last, 1, 0)
    pl.semaphore_wait(barrier, len(row_peers) + beside)

    own_a.wait()

    def own_acts(k, act):
        @pl.when(c < last)
        def _():
            act(act_copy(c, 1, k))

        @pl.when(c > 0)
        def _():
            act(act_copy(c, 0, k))

    for k in range(n_a):
        own_acts(k, lambda copy: copy.start())
    own_w.wait()
    for k in range(n_w):
        for slot, to in enumerate(row_peers):
            weight_copy(r, to, slot, k).start()

    near = [row_of(*p) for p in peers_x + peers_y]
    far = [row_of(*p) for p in diagonal]
    base_relay = len(row_peers)
    base_share = base_relay + len(diagonal)

    def relays(k, act):
        for n, (dy, dx) in enumerate(diagonal):
            @pl.when(core == 0)
            def _():
                act(weight_copy(row_of(dy, 0), row_of(0, dx), base_relay + n, k))

            @pl.when(core == 1)
            def _():
                act(weight_copy(row_of(0, dx), row_of(dy, 0), base_relay + n, k))

    def wait_weight(source, k):
        weight_copy(source, r, 0, k).wait_recv()

    def first_weights(k):
        for source in near:
            wait_weight(source, k)
        relays(k, lambda copy: copy.start())
        for n, source in enumerate(near):
            weight_copy(source, pair, base_share + n, k).start()

    def far_weights(k):
        for n, source in enumerate(far):
            wait_weight(source, k)
            weight_copy(source, pair, base_share + len(near) + n, k).start()

    short = jnp.minimum(c, last - c)
    toward = jnp.where(last - c >= c, 1, -1)

    def source_at(t):
        near_step = t // 2 + 1
        near_sign = toward * (1 - 2 * lax.rem(t, 2))
        return jnp.where(t < 2 * short, c + near_sign * near_step, c + toward * (t - short + 1))

    inner = jnp.logical_and(c > 0, c < last)

    def pass_acts(t, k):
        source = source_at(t)
        act_copy(source, 0, k).wait_recv()

        @pl.when(source < c)
        def _():
            act_copy(source, 1, k).start()

        @pl.when(source > c)
        def _():
            act_copy(source, 0, k).start()

    events = []
    a_time, w_time = row_a * width, row_w * weights.shape[2]
    for t in range(last):
        for k in range(n_a):
            events.append(((t // 2 * n_a + k + 1) * a_time, "a", t, k))
    for k in range(n_w):
        events.append(((k + 1) * w_time * (n_x + n_y - 2) / 2, "near", 0, k))
        events.append(((k + 2) * w_time * (n_x + n_y - 2) / 2 + w_time, "far", 0, k))
    for _, kind, t, k in sorted(events):
        if kind == "a":
            pl.when(inner)(functools.partial(pass_acts, t, k))
        elif kind == "near":
            first_weights(k)
        else:
            far_weights(k)
    for k in range(n_w):
        for source in [pair] + [row_of(dy, dx, True) for dy, dx in peers_x + peers_y + diagonal]:
            wait_weight(source, k)

    def product(source, rows):
        at = lax.rem(source - c + n_col, n_col)
        return jnp.dot(acts[source, rows, :], weights[at], preferred_element_type=jnp.float32)

    every = pl.ds(0, tokens)
    total[...] = product(c, every)

    @pl.loop(0, last - 1)
    def _(t):
        source = source_at(t)

        @pl.when(jnp.logical_not(inner))
        def _():
            for k in range(n_a):
                act_copy(source, 0, k).wait_recv()

        total[...] += product(source, every)

    final = source_at(last - 1)

    @pl.loop(0, n_a)
    def _(k):
        rows = pl.ds(pl.multiple_of(k * row_a, row_a), row_a)

        @pl.when(jnp.logical_not(inner))
        def _():
            act_copy(final, 0, k).wait_recv()

        pre = total[rows, :] + product(final, rows)
        out[rows, :] = (pre / (1.0 + jnp.exp(-pre))).astype(out.dtype)

    for k in range(n_a):
        own_acts(k, lambda copy: copy.wait_send())

    @pl.when(inner)
    def _():
        @pl.loop(0, last)
        def _(t):
            source = source_at(t)
            for k in range(n_a):
                @pl.when(source < c)
                def _():
                    act_copy(source, 1, k).wait_send()

                @pl.when(source > c)
                def _():
                    act_copy(source, 0, k).wait_send()

    for k in range(n_w):
        for slot, to in enumerate(row_peers):
            weight_copy(r, to, slot, k).wait_send()
        relays(k, lambda copy: copy.wait_send())
        for n, source in enumerate(near + far):
            weight_copy(source, pair, base_share + n, k).wait_send()


def body(n_row, n_col, act_tiles, up_tiles):
    tokens, width = act_tiles.shape
    depth, hidden = up_tiles.shape
    chips = n_row // 2
    n_x = max(n for n in range(1, chips + 1) if chips % n == 0 and n * n <= chips)
    n_y = chips // n_x
    n_a, n_w = pieces_of(tokens, 4, 16), pieces_of(depth, 2, 16)
    sends = (n_x - 1) + (n_y - 1) + 1 + (n_x - 1) * (n_y - 1) + chips - 1
    return pl.pallas_call(
        functools.partial(kernel, (n_y, n_x, n_col), (n_a, n_w)),
        out_shape=jax.ShapeDtypeStruct((tokens, hidden), jnp.bfloat16),
        in_specs=[pl.BlockSpec(memory_space=pltpu.HBM)] * 2,
        out_specs=pl.BlockSpec(memory_space=pltpu.VMEM),
        scratch_shapes=[
            pltpu.VMEM((n_col, tokens, width), jnp.bfloat16),
            pltpu.VMEM((n_row * depth // width, width, hidden), jnp.bfloat16),
            pltpu.VMEM((tokens, hidden), jnp.float32),
            pltpu.SemaphoreType.DMA((2, n_col, n_a)),
            pltpu.SemaphoreType.DMA((n_col, n_a)),
            pltpu.SemaphoreType.DMA((sends, n_w)),
            pltpu.SemaphoreType.DMA((n_row, n_w)),
            pltpu.SemaphoreType.DMA((2,)),
        ],
        compiler_params=pltpu.CompilerParams(collective_id=0, has_side_effects=True, vmem_limit_bytes=48 << 20),
        cost_estimate=pl.CostEstimate(
            flops=2 * tokens * width * n_col * hidden,
            bytes_accessed=2 * (act_tiles.size + up_tiles.size + tokens * hidden),
            transcendentals=tokens * hidden,
        ),
        name="gather_up_silu",
    )(act_tiles, up_tiles)


def solution(mesh):
    return jax.shard_map(
        functools.partial(body, mesh.shape["row"], mesh.shape["col"]),
        mesh=mesh,
        in_specs=(P("row", "col"), P("row", "col")),
        out_specs=P("row", "col"),
        check_vma=False,
    )
```

time: 86.7 us -> 34.9 us (0.40)
  waiting for transfers between devices: 58.5 us -> 0 us
  Pallas kernels: 0 us -> 31.9 us
  starting transfers between devices: 17.7 us -> 0 us
  local copies, waits for them, and re-layouts: 6.35 us -> 2.86 us
  matrix products: 2.59 us -> 0 us
  other arithmetic: 1.21 us -> 0 us
    ppermute x7 -> x0, waiting for transfers between devices: 58.5 us -> none  [passed_along(): return lax.ppermute(block, axis, route)]
    pallas_call x0 -> x1, Pallas kernels: none -> 31.9 us  [body(): pl.pallas_call(functools.partial(kernel, (n_y, n_x, n_col), (n_a, n_w)),...]
    ppermute x7 -> x0, starting transfers between devices: 17.7 us -> none  [passed_along(): return lax.ppermute(block, axis, route)]
    while x7 -> x0, local copies, waits for them, and re-layouts: 3.3 us -> none
    dot_general x4 -> x0, matrix products: 2.59 us -> none  [the longest x3 1.92 us: advance(): jnp.dot(act_now, pair_now, preferred_element_type=jnp.float32)]
    convert_element_type x1 -> x0, other arithmetic: 1.21 us -> none  [body(): return jax.nn.silu(summed).astype(jnp.bfloat16)]
    unnamed x4 -> x5, local copies, waits for them, and re-layouts: 3.01 us -> 2.86 us
  transfers between devices with their start and end apart: 7 -> 0, of which waited for: 7 -> 0; matrix products, arithmetic and copies ran while one was open for 1% -> 0% of each run, Pallas kernels for 0% -> 0%
where the time goes in v1:
time: 34.9 us; the launch traced here: 34.7 us
  Pallas kernels  31.9 us (91%)
  local copies, waits for them, and re-layouts  2.86 us (8%)
    pallas_call x1, Pallas kernels, body(): pl.pallas_call(functools.partial(kernel, (n_y, n_x, n_col), (n_a, n_w)),...  31.9 us
    unnamed x5, local copies, waits for them, and re-layouts  2.86 us

profile of v1, /device:TPU:0, one launch (start us, length us, event | category | flops | bytes accessed | tf_op | source)
XLA Modules:
  0.0 34.7 jit_solution(14324774233149235997)
XLA Ops:
  0.0 0.0 copy-start
  0.0 1.0 %copy-done = bf16[256,896]{1,0:T(8,128)(2,1)S(1)} copy-done((bf16[256,896]{1,0:T(8,128)(2,1)S(1)}, bf16[256,896]{1,0:T(8,128)(2,1)}, u32[]{:S(2)}) %copy-start) | copy-done | bytes 458776
  1.0 0.0 copy-start.1
  1.0 1.0 %copy-done.1 = bf16[384,512]{1,0:T(8,128)(2,1)S(1)} copy-done((bf16[384,512]{1,0:T(8,128)(2,1)S(1)}, bf16[384,512]{1,0:T(8,128)(2,1)}, u32[]{:S(2)}) %copy-start.1) | copy-done | bytes 393240
  2.0 31.9 %gather_up_silu.1 = bf16[384,896]{1,0:T(8,128)(2,1)S(1)} custom-call(bf16[384,512]{1,0:T(8,128)(2,1)S(1)} %copy-done.1, bf16[256,896]{1,0:T(8,128)(2,1)S(1)} %copy-done), custom_call_target="tpu_custom_call" | custom-call | flops 1409286144 | bytes 1540096 | tf_op jit(solution)/shard_map/gather_up_silu/pallas_call | solution.py:239
  33.9 0.8 %copy.4 = bf16[384,896]{1,0:T(8,128)(2,1)} copy(bf16[384,896]{1,0:T(8,128)(2,1)S(1)} %gather_up_silu.1) | data formatting | bytes 1376256
Async XLA Ops:
  0.0 1.0 %copy-start = (bf16[256,896]{1,0:T(8,128)(2,1)S(1)}, bf16[256,896]{1,0:T(8,128)(2,1)}, u32[]{:S(2)}) copy-start(bf16[256,896]{1,0:T(8,128)(2,1)} %w_hbm.1) | copy-start | bytes 1376260
  1.0 1.0 %copy-start.1 = (bf16[384,512]{1,0:T(8,128)(2,1)S(1)}, bf16[384,512]{1,0:T(8,128)(2,1)}, u32[]{:S(2)}) copy-start(bf16[384,512]{1,0:T(8,128)(2,1)} %a_hbm.1) | copy-start | bytes 1179652

commit v2 on v1

--- a/solution.py
+++ b/solution.py
@@ -42,9 +42,9 @@
         rel = lax.rem(source - owner + n_row, n_row)
         return weights.at[rel // per, pl.ds(pl.multiple_of(lax.rem(rel, per) * depth + k * row_w, row_w), row_w)]
 
-    def weight_copy(source, to, slot, k):
+    def weight_copy(source, to, slot, k, own=False):
         return pltpu.make_async_remote_copy(
-            src_ref=weight_at(source, r, k),
+            src_ref=w_hbm.at[pl.ds(k * row_w, row_w)] if own else weight_at(source, r, k),
             dst_ref=weight_at(source, to, k),
             send_sem=send_w.at[slot, k],
             recv_sem=recv_w.at[source, k],
@@ -52,9 +52,9 @@
             device_id_type=MESH,
         )
 
-    def act_copy(source, side, k):
+    def act_copy(source, side, k, own=False):
         return pltpu.make_async_remote_copy(
-            src_ref=acts.at[source, pl.ds(k * row_a, row_a)],
+            src_ref=(a_hbm if own else acts.at[source]).at[pl.ds(k * row_a, row_a)],
             dst_ref=acts.at[source, pl.ds(k * row_a, row_a)],
             send_sem=send_a.at[side, source, k],
             recv_sem=recv_a.at[source, k],
@@ -83,23 +83,20 @@
     beside = jnp.where(c > 0, 1, 0) + jnp.where(c < last, 1, 0)
     pl.semaphore_wait(barrier, len(row_peers) + beside)
 
-    own_a.wait()
-
     def own_acts(k, act):
         @pl.when(c < last)
         def _():
-            act(act_copy(c, 1, k))
+            act(act_copy(c, 1, k, True))
 
         @pl.when(c > 0)
         def _():
-            act(act_copy(c, 0, k))
+            act(act_copy(c, 0, k, True))
 
     for k in range(n_a):
         own_acts(k, lambda copy: copy.start())
-    own_w.wait()
     for k in range(n_w):
         for slot, to in enumerate(row_peers):
-            weight_copy(r, to, slot, k).start()
+            weight_copy(r, to, slot, k, True).start()
 
     near = [row_of(*p) for p in peers_x + peers_y]
     far = [row_of(*p) for p in diagonal]
@@ -176,6 +173,8 @@
         at = lax.rem(source - c + n_col, n_col)
         return jnp.dot(acts[source, rows, :], weights[at], preferred_element_type=jnp.float32)
 
+    own_a.wait()
+    own_w.wait()
     every = pl.ds(0, tokens)
     total[...] = product(c, every)
 
@@ -222,7 +221,7 @@
 
     for k in range(n_w):
         for slot, to in enumerate(row_peers):
-            weight_copy(r, to, slot, k).wait_send()
+            weight_copy(r, to, slot, k, True).wait_send()
         relays(k, lambda copy: copy.wait_send())
         for n, source in enumerate(near + far):
             weight_copy(source, pair, base_share + n, k).wait_send()
@@ -238,7 +237,7 @@
     sends = (n_x - 1) + (n_y - 1) + 1 + (n_x - 1) * (n_y - 1) + chips - 1
     return pl.pallas_call(
         functools.partial(kernel, (n_y, n_x, n_col), (n_a, n_w)),
-        out_shape=jax.ShapeDtypeStruct((tokens, hidden), jnp.bfloat16),
+        out_shape=pltpu.VMEM((tokens, hidden), jnp.bfloat16),
         in_specs=[pl.BlockSpec(memory_space=pltpu.HBM)] * 2,
         out_specs=pl.BlockSpec(memory_space=pltpu.VMEM),
         scratch_shapes=[
@@ -251,7 +250,7 @@
             pltpu.SemaphoreType.DMA((n_row, n_w)),
             pltpu.SemaphoreType.DMA((2,)),
         ],
-        compiler_params=pltpu.CompilerParams(collective_id=0, has_side_effects=True, vmem_limit_bytes=48 << 20),
+        compiler_params=pltpu.CompilerParams(collective_id=0, has_side_effects=True, vmem_limit_bytes=60000000),
         cost_estimate=pl.CostEstimate(
             flops=2 * tokens * width * n_col * hidden,
             bytes_accessed=2 * (act_tiles.size + up_tiles.size + tokens * hidden),

time: 34.9 us -> 32.6 us (0.934)
  local copies, waits for them, and re-layouts: 2.86 us -> 0.85 us
    unnamed x5 -> x1, local copies, waits for them, and re-layouts: 2.86 us -> 0.85 us
where the time goes in v2:
time: 32.6 us; the launch traced here: 32.5 us
  Pallas kernels  31.6 us (97%)
  local copies, waits for them, and re-layouts  0.85 us (3%)
    pallas_call x1, Pallas kernels, body(): pl.pallas_call(functools.partial(kernel, (n_y, n_x, n_col), (n_a, n_w)),...  31.6 us
    unnamed x1, local copies, waits for them, and re-layouts  0.85 us

profile of v2, /device:TPU:0, one launch (start us, length us, event | category | flops | bytes accessed | tf_op | source)
XLA Modules:
  0.0 32.5 jit_solution(7059983854921647634)
XLA Ops:
  0.0 31.6 %gather_up_silu.1 = bf16[384,896]{1,0:T(8,128)(2,1)S(1)} custom-call(bf16[384,512]{1,0:T(8,128)(2,1)} %a_hbm.1, bf16[256,896]{1,0:T(8,128)(2,1)} %w_hbm.1), custom_call_target="tpu_custom_call" | custom-call | flops 1409286144 | bytes 1540096 | tf_op jit(solution)/shard_map/gather_up_silu/pallas_call | solution.py:238
  31.6 0.8 %copy.4 = bf16[384,896]{1,0:T(8,128)(2,1)} copy(bf16[384,896]{1,0:T(8,128)(2,1)S(1)} %gather_up_silu.1) | data formatting | bytes 1376256

commit v3 on v1

--- a/solution.py
+++ b/solution.py
@@ -12,6 +12,14 @@
 
 def pieces_of(rows, wanted, multiple):
     return max(n for n in range(1, wanted + 1) if rows % (n * multiple) == 0)
+
+
+def pieces_halved(rows, wanted, multiple):
+    pieces = []
+    while len(pieces) < wanted - 1 and rows % (2 * multiple) == 0:
+        rows //= 2
+        pieces.append(rows)
+    return pieces + [rows]
 
 
 def kernel(grid, counts, a_hbm, w_hbm, out, acts, weights, total, send_a, recv_a, send_w, recv_w, local_sem):
@@ -21,7 +29,9 @@
     tokens, width = acts.shape[1:]
     depth = w_hbm.shape[0]
     per = width // depth
-    row_a, row_w = tokens // n_a, depth // n_w
+    row_w = depth // n_w
+    starts_a = [sum(n_a[:k]) for k in range(len(n_a))]
+    sizes_a, n_a = n_a, len(n_a)
 
     r, c = lax.axis_index("row"), lax.axis_index("col")
     core = lax.rem(r, 2)
@@ -54,8 +64,8 @@
 
     def act_copy(source, side, k):
         return pltpu.make_async_remote_copy(
-            src_ref=acts.at[source, pl.ds(k * row_a, row_a)],
-            dst_ref=acts.at[source, pl.ds(k * row_a, row_a)],
+            src_ref=acts.at[source].at[pl.ds(starts_a[k], sizes_a[k])],
+            dst_ref=acts.at[source, pl.ds(starts_a[k], sizes_a[k])],
             send_sem=send_a.at[side, source, k],
             recv_sem=recv_a.at[source, k],
             device_id=(r, c + 2 * side - 1),
@@ -83,8 +93,6 @@
     beside = jnp.where(c > 0, 1, 0) + jnp.where(c < last, 1, 0)
     pl.semaphore_wait(barrier, len(row_peers) + beside)
 
-    own_a.wait()
-
     def own_acts(k, act):
         @pl.when(c < last)
         def _():
@@ -94,6 +102,7 @@
         def _():
             act(act_copy(c, 0, k))
 
+    own_a.wait()
     for k in range(n_a):
         own_acts(k, lambda copy: copy.start())
     own_w.wait()
@@ -154,7 +163,7 @@
             act_copy(source, 0, k).start()
 
     events = []
-    a_time, w_time = row_a * width, row_w * weights.shape[2]
+    a_time, w_time = tokens // n_a * width, row_w * weights.shape[2]
     for t in range(last):
         for k in range(n_a):
             events.append(((t // 2 * n_a + k + 1) * a_time, "a", t, k))
@@ -192,13 +201,10 @@
 
     final = source_at(last - 1)
 
-    @pl.loop(0, n_a)
-    def _(k):
-        rows = pl.ds(pl.multiple_of(k * row_a, row_a), row_a)
-
-        @pl.when(jnp.logical_not(inner))
-        def _():
-            act_copy(final, 0, k).wait_recv()
+    for k in range(n_a):
+        rows = pl.ds(starts_a[k], sizes_a[k])
+
+        pl.when(jnp.logical_not(inner))(act_copy(final, 0, k).wait_recv)
 
         pre = total[rows, :] + product(final, rows)
         out[rows, :] = (pre / (1.0 + jnp.exp(-pre))).astype(out.dtype)
@@ -234,11 +240,12 @@
     chips = n_row // 2
     n_x = max(n for n in range(1, chips + 1) if chips % n == 0 and n * n <= chips)
     n_y = chips // n_x
-    n_a, n_w = pieces_of(tokens, 4, 16), pieces_of(depth, 2, 16)
+    cuts, n_w = pieces_halved(tokens, 3, 16), pieces_of(depth, 1, 16)
+    n_a = len(cuts)
     sends = (n_x - 1) + (n_y - 1) + 1 + (n_x - 1) * (n_y - 1) + chips - 1
     return pl.pallas_call(
-        functools.partial(kernel, (n_y, n_x, n_col), (n_a, n_w)),
-        out_shape=jax.ShapeDtypeStruct((tokens, hidden), jnp.bfloat16),
+        functools.partial(kernel, (n_y, n_x, n_col), (cuts, n_w)),
+        out_shape=pltpu.VMEM((tokens, hidden), jnp.bfloat16),
         in_specs=[pl.BlockSpec(memory_space=pltpu.HBM)] * 2,
         out_specs=pl.BlockSpec(memory_space=pltpu.VMEM),
         scratch_shapes=[
@@ -251,7 +258,7 @@
             pltpu.SemaphoreType.DMA((n_row, n_w)),
             pltpu.SemaphoreType.DMA((2,)),
         ],
-        compiler_params=pltpu.CompilerParams(collective_id=0, has_side_effects=True, vmem_limit_bytes=48 << 20),
+        compiler_params=pltpu.CompilerParams(collective_id=0, has_side_effects=True, vmem_limit_bytes=60000000),
         cost_estimate=pl.CostEstimate(
             flops=2 * tokens * width * n_col * hidden,
             bytes_accessed=2 * (act_tiles.size + up_tiles.size + tokens * hidden),

time: 34.9 us -> 32.1 us (0.920)
  local copies, waits for them, and re-layouts: 2.86 us -> 0.85 us
  Pallas kernels: 31.9 us -> 31.1 us
    unnamed x5 -> x1, local copies, waits for them, and re-layouts: 2.86 us -> 0.85 us
    pallas_call x1, Pallas kernels: 31.9 us -> 31.1 us  [body(): pl.pallas_call(functools.partial(kernel, (n_y, n_x, n_col), (cuts, n_w)),...]
where the time goes in v3:
time: 32.1 us; the launch traced here: 32 us
  Pallas kernels  31.1 us (97%)
  local copies, waits for them, and re-layouts  0.85 us (3%)
    pallas_call x1, Pallas kernels, body(): pl.pallas_call(functools.partial(kernel, (n_y, n_x, n_col), (cuts, n_w)),...  31.1 us
    unnamed x1, local copies, waits for them, and re-layouts  0.85 us

profile of v3, /device:TPU:0, one launch (start us, length us, event | category | flops | bytes accessed | tf_op | source)
XLA Modules:
  0.0 32.0 jit_solution(3702535011681930971)
XLA Ops:
  0.0 31.1 %gather_up_silu.1 = bf16[384,896]{1,0:T(8,128)(2,1)S(1)} custom-call(bf16[384,512]{1,0:T(8,128)(2,1)} %a_hbm.1, bf16[256,896]{1,0:T(8,128)(2,1)} %w_hbm.1), custom_call_target="tpu_custom_call" | custom-call | flops 1409286144 | bytes 1540096 | tf_op jit(solution)/shard_map/gather_up_silu/pallas_call | solution.py:246
  31.1 0.8 %copy.4 = bf16[384,896]{1,0:T(8,128)(2,1)} copy(bf16[384,896]{1,0:T(8,128)(2,1)S(1)} %gather_up_silu.1) | data formatting | bytes 1376256

commit v4 on v3

--- a/solution.py
+++ b/solution.py
@@ -79,9 +79,6 @@
 
     barrier = pltpu.get_barrier_semaphore()
     row_peers = [row_of(*p) for p in peers_x + peers_y] + [pair]
-    for to in row_peers:
-        pl.semaphore_signal(barrier, inc=1, device_id=(to, c), device_id_type=MESH)
-
     @pl.when(c > 0)
     def _():
         pl.semaphore_signal(barrier, inc=1, device_id=(r, c - 1), device_id_type=MESH)
@@ -89,6 +86,9 @@
     @pl.when(c < last)
     def _():
         pl.semaphore_signal(barrier, inc=1, device_id=(r, c + 1), device_id_type=MESH)
+
+    for to in row_peers:
+        pl.semaphore_signal(barrier, inc=1, device_id=(to, c), device_id_type=MESH)
 
     beside = jnp.where(c > 0, 1, 0) + jnp.where(c < last, 1, 0)
     pl.semaphore_wait(barrier, len(row_peers) + beside)

time: 32.1 us -> 32.1 us (level)
  no operation moved by 1% of the time
where the time goes in v4:
time: 32.1 us; the launch traced here: 32 us
  Pallas kernels  31.1 us (97%)
  local copies, waits for them, and re-layouts  0.85 us (3%)
    pallas_call x1, Pallas kernels, body(): pl.pallas_call(functools.partial(kernel, (n_y, n_x, n_col), (cuts, n_w)),...  31.1 us
    unnamed x1, local copies, waits for them, and re-layouts  0.85 us

profile of v4, /device:TPU:0, one launch (start us, length us, event | category | flops | bytes accessed | tf_op | source)
XLA Modules:
  0.0 32.0 jit_solution(4770040455863970132)
XLA Ops:
  0.0 31.1 %gather_up_silu.1 = bf16[384,896]{1,0:T(8,128)(2,1)S(1)} custom-call(bf16[384,512]{1,0:T(8,128)(2,1)} %a_hbm.1, bf16[256,896]{1,0:T(8,128)(2,1)} %w_hbm.1), custom_call_target="tpu_custom_call" | custom-call | flops 1409286144 | bytes 1540096 | tf_op jit(solution)/shard_map/gather_up_silu/pallas_call | solution.py:246
  31.1 0.8 %copy.4 = bf16[384,896]{1,0:T(8,128)(2,1)} copy(bf16[384,896]{1,0:T(8,128)(2,1)S(1)} %gather_up_silu.1) | data formatting | bytes 1376256
